TPU v7x, 256 devices: a whole 4x4x8 slice. The times are simulated.
256 devices in a mesh: expert: 32 (over y, z), unit: 8 (over x, core).
Axes of the slice: x: 4, y: 4, z: 8, core: 2. Of those that a mesh axis runs over, the one named last changes fastest.
Arguments:
- w_up: bfloat16 [128, 1536, 4096], P('expert', 'unit'), may hold values from -0.09375 to 0.09375
- cluster: int32 [128, 1], replicated, may hold values from 0 to 31
- counts: int32 [128], replicated, may hold values from 16 to 127
Outputs:
- merged: bfloat16 [32, 1536, 4096], P('expert', None, 'unit')
Inputs may be any that keep to these rules, and one draw needn't show every extreme that they name: Every cluster has at least one member.
All inputs are finite; a program needn't handle non-finite values.
Results may differ from a plain program's by a relative error of at most 0.0051.
Values may be sent and summed in bfloat16 or wider, within the bound.
No kernel may reach another device: no remote copies, remote signals or barrier semaphores. Data moves between devices by JAX's collectives and lax.ppermute only.
A program may use at most 128 MiB of HBM per device.

v0:
```python
import jax
import jax.numpy as jnp
from jax import lax
from jax.sharding import PartitionSpec as P

BLOCK = 96
NS_STEPS = 8
CLU_DEV = 1


def newton_schulz(matrices):
    frob_norm = jnp.sqrt(jnp.sum(matrices * matrices, axis=(-2, -1), keepdims=True) + 1e-06)
    value = matrices / frob_norm
    for iteration in range(NS_STEPS):
        square = jnp.einsum("...ij,...kj->...ik", value, value, precision=lax.Precision.HIGHEST)
        value = 1.5 * value - 0.5 * jnp.einsum(
            "...ik,...kj->...ij", square, value, precision=lax.Precision.HIGHEST
        )
    return value


def block_gram(left, right):
    experts, units, width = left.shape
    nblocks = units // BLOCK
    lead_rows = left.reshape(experts, nblocks, BLOCK, width)
    member_rows = right.reshape(experts, nblocks, BLOCK, width)
    gram = jnp.einsum("nbid,nbjd->nibj", lead_rows, member_rows, preferred_element_type=jnp.float32)
    return gram.reshape(experts, BLOCK, units)


def polar_factors(gram):
    experts, height, units = gram.shape
    nblocks = units // BLOCK
    matrices = gram.reshape(experts, BLOCK, nblocks, BLOCK).transpose(0, 2, 1, 3)
    polar = newton_schulz(matrices).astype(jnp.bfloat16)
    return polar.transpose(0, 2, 1, 3).reshape(experts, BLOCK, units)


def align_rows(factors, slab, scale):
    experts, units, width = slab.shape
    nblocks = units // BLOCK
    turn = factors.reshape(experts, BLOCK, nblocks, BLOCK)
    member_rows = slab.reshape(experts, nblocks, BLOCK, width)
    turned = jnp.einsum("nibj,nbjd->nbid", turn, member_rows, preferred_element_type=jnp.float32)
    turned = turned * scale[:, None, None, None]
    return turned.reshape(experts, units, width).astype(jnp.bfloat16)


def on_device(w_up, cluster, counts):
    cluster_ids = cluster[:, 0]
    experts = cluster_ids.shape[0]
    clusters = CLU_DEV * lax.axis_size("expert")
    index = jnp.arange(experts, dtype=jnp.int32)
    labels = jnp.arange(clusters, dtype=jnp.int32)
    member = cluster_ids[None, :] == labels[:, None]
    score = counts * experts + (experts - 1 - index)
    best = jnp.max(jnp.where(member, score[None, :], -1), axis=1)
    leader = experts - 1 - best % experts
    anchor_of = jnp.sum(jnp.where(member, leader[:, None], 0), axis=0)
    total = jnp.sum(jnp.where(member, counts[None, :], 0), axis=1).astype(jnp.float32)
    weight = counts.astype(jnp.float32) / jnp.sum(jnp.where(member, total[:, None], 0.0), axis=0)
    columns = lax.all_to_all(w_up, "expert", split_axis=2, concat_axis=0, tiled=True)
    anchors = jnp.take(columns, anchor_of, axis=0)
    gram = lax.psum_scatter(block_gram(anchors, columns), "expert", scatter_dimension=0, tiled=True)
    polar = polar_factors(gram)
    aligned = align_rows(lax.all_gather(polar, "expert", axis=0, tiled=True), columns, weight)
    select = member.astype(jnp.bfloat16)
    summed = jnp.dot(select, aligned.reshape(experts, -1), preferred_element_type=jnp.float32)
    merged = summed.reshape(clusters, aligned.shape[1], aligned.shape[2]).astype(jnp.bfloat16)
    return lax.all_to_all(
        lax.all_to_all(merged, "expert", split_axis=0, concat_axis=2, tiled=True),
        "unit",
        split_axis=2,
        concat_axis=1,
        tiled=True,
    )


def solution(mesh):
    return jax.shard_map(
        on_device,
        mesh=mesh,
        in_specs=(P("expert", "unit", None), P(), P()),
        out_specs=P("expert", None, "unit"),
        check_vma=False,
    )
```

profile of v0, /device:TPU:1, one launch (start us, length us, event | category | flops | bytes accessed | tf_op | source)
XLA Modules:
  0.0 799.8 jit_solution(10294570698834870266)
XLA Ops:
  6.5 13.1 %copy.44 = bf16[4,192,4096]{1,0,2:T(4,128)(2,1)} copy(bf16[4,192,4096]{2,1,0:T(8,128)(2,1)} %param.3) | data formatting | bytes 12582912 | tf_op args[0]
  19.6 12.3 %all-to-all-start = ((bf16[4,192,4096]{1,0,2:T(4,128)(2,1)}), bf16[4,192,4096]{1,0,2:T(4,128)(2,1)}, u32[]{:S(2)}, u32[]{:S(2)}) async-start(bf16[4,192,4096]{1,0,2:T(4,128)(2,1)} %copy.44), calls=%async_computation | async-start | bytes 16777216 | tf_op jit(solution)/shard_map/all_to_all | solution.py:62
  32.3 187.8 %all-to-all-done = bf16[4,192,4096]{1,0,2:T(4,128)(2,1)} async-done(((bf16[4,192,4096]{1,0,2:T(4,128)(2,1)}), bf16[4,192,4096]{1,0,2:T(4,128)(2,1)}, u32[]{:S(2)}, u32[]{:S(2)}) %all-to-all-start) | async-done | bytes 6291488 | tf_op jit(solution)/shard_map/all_to_all | solution.py:62
  220.1 13.2 %copy.45 = bf16[4,192,32,128]{3,1,0,2:T(8,128)(2,1)} copy(bf16[4,192,32,128]{1,0,3,2:T(4,128)(2,1)} %bitcast.2) | data formatting | bytes 12582912 | tf_op jit(solution)/shard_map/all_to_all | solution.py:62
  233.3 6.7 gather_fusion
  240.0 13.4 %fusion.3 = f32[128,96,2,96]{3,1,2,0:T(8,128)} fusion(bf16[128,2,96,128]{3,2,1,0:T(8,128)(2,1)} %bitcast.128, bf16[128,2,96,128]{3,2,1,0:T(8,128)(2,1)} %bitcast.134, pred[128]{0:T(512)(128)(4,1)S(1)} %compare_and_fusion), kind=kOutput, calls=%fused_computation.6 | convolution fusion | flops 607125504 | bytes 22020224 | tf_op jit(solution)/shard_map/nbid,nbjd->nibj/dot_general | solution.py:27
  253.5 11.7 %copy.46 = f32[128,96,2,96]{0,3,2,1:T(8,128)} copy(f32[128,96,2,96]{3,1,2,0:T(8,128)} %fusion.3) | data formatting | bytes 18874368 | tf_op jit(solution)/shard_map/nbid,nbjd->nibj/transpose | solution.py:27
  265.2 12.7 %copy.47 = f32[128,96,192]{2,1,0:T(8,128)} copy(f32[128,96,192]{0,2,1:T(8,128)} %bitcast.130) | data formatting | bytes 18874368 | tf_op jit(solution)/shard_map/reshape | solution.py:28
  278.1 237.5 %reduce-scatter.2.cloned.1.call-done = f32[4,96,192]{2,1,0:T(8,128)} async-done(((f32[128,96,192]{2,1,0:T(8,128)}), f32[4,96,192]{2,1,0:T(8,128)}) %reduce-scatter.2.cloned.1.call-update) | async-done | bytes 294928 | tf_op jit(solution)/shard_map/reduce_scatter | solution.py:64
  515.6 1.2 copy.48
  517.1 1.0 fusion.18
  520.2 0.9 fusion.34
  523.1 0.9 fusion.35
  524.6 0.9 fusion.38
  526.0 0.9 fusion.33
  527.5 1.0 fusion.21
  530.4 90.1 %all-gather.2.cloned.1.call-done = bf16[128,96,192]{2,1,0:T(8,128)(2,1)} async-done(((bf16[4,96,192]{2,1,0:T(8,128)(2,1)}), bf16[128,96,192]{2,1,0:T(8,128)(2,1)}) %all-gather.2.cloned.1.call-update) | async-done | bytes 4718608 | tf_op jit(solution)/shard_map/all_gather | solution.py:66
  620.5 8.8 %copy.52 = bf16[128,96,192]{0,2,1:T(8,128)(2,1)} copy(bf16[128,96,192]{2,1,0:T(8,128)(2,1)} %all-gather.2.cloned.1.call-done) | data formatting | bytes 9437184 | tf_op jit(solution)/shard_map/all_gather | solution.py:66
  629.2 8.5 %copy.53 = bf16[128,96,2,96]{3,1,2,0:T(8,128)(2,1)} copy(bf16[128,96,2,96]{0,3,2,1:T(8,128)(2,1)} %bitcast.135) | data formatting | bytes 9437184 | tf_op jit(solution)/shard_map/reshape | solution.py:42
  637.7 6.4 multiply_convert_fusion
  644.1 8.0 %copy.65 = bf16[16,8,192,128]{3,1,2,0:T(8,128)(2,1)} copy(bf16[16,8,192,128]{3,2,1,0:T(8,128)(2,1)S(1)} %bitcast.133) | data formatting | bytes 12582912
  652.2 8.6 %copy.54 = bf16[24576,128]{1,0:T(8,128)(2,1)} copy(bf16[24576,128]{0,1:T(8,128)(2,1)} %bitcast.131) | data formatting | bytes 12582912 | tf_op jit(solution)/shard_map/dot_general | solution.py:68
  660.8 4.9 convolution_convert_fusion
  666.4 41.9 %all_to_all.54 = bf16[32,192,128]{2,1,0:T(8,128)(2,1)} all-to-all(bf16[32,192,128]{2,1,0:T(8,128)(2,1)S(1)} %copy.55), channel_id=1, replica_groups=mesh['expert'=32,'unit'=8] {'expert'}, dimensions={0} | all-to-all | bytes 3145728 | tf_op jit(solution)/shard_map/all_to_all | solution.py:71
  708.3 3.1 copy.60
  711.4 6.2 reshape.84
  718.1 23.6 %reduce.1 = bf16[4096,192]{1,0:T(8,128)(2,1)S(1)} reduce(bf16[4096,1,192]{2,1,0:T(2,128)(2,1)} %bitcast.136, bf16[]{:T(256)} %broadcast.142), dimensions={1}, to_apply=%bitcast.99.reduce_sub_computation | reduce | bytes 3145730
  741.8 4.4 reshape.85
  746.1 29.5 %all_to_all.55 = bf16[8,2,49152]{2,1,0:T(2,128)(2,1)S(1)} all-to-all(bf16[8,2,49152]{2,1,0:T(2,128)(2,1)} %reshape.85), channel_id=1, replica_groups=mesh['expert'=32,'unit'=8] {'unit'}, dimensions={0} | all-to-all | bytes 3145728 | tf_op jit(solution)/shard_map/all_to_all | solution.py:70
  775.7 4.9 reshape.86
  780.6 9.9 %copy.58 = bf16[1,192,4096]{2,1,0:T(8,128)(2,1)S(1)} copy(bf16[1,192,4096]{1,0,2:T(2,128)(2,1)} %bitcast.137) | data formatting | bytes 3145728 | tf_op jit(solution)/shard_map/all_to_all | solution.py:70
  791.3 1.6 copy.59
  (37 shorter events, 10.3 us)
Async XLA Ops:
  19.6 12.3 %copy-start.1 = (s32[128]{0:T(128)S(1)}, s32[128]{0:T(128)}, u32[]{:S(2)}) copy-start(s32[128]{0:T(128)} %param.5) | copy-start | bytes 1540
  19.6 12.4 %copy-start = (s32[128,1]{0,1:T(1,128)S(1)}, s32[128,1]{0,1:T(1,128)}, u32[]{:S(2)}) copy-start(s32[128,1]{0,1:T(1,128)} %param.4) | copy-start | bytes 1540
  19.6 200.5 %all-to-all-start = ((bf16[4,192,4096]{1,0,2:T(4,128)(2,1)}), bf16[4,192,4096]{1,0,2:T(4,128)(2,1)}, u32[]{:S(2)}, u32[]{:S(2)}) async-start(bf16[4,192,4096]{1,0,2:T(4,128)(2,1)} %copy.44), calls=%async_computation | async-start | bytes 16777216 | tf_op jit(solution)/shard_map/all_to_all | solution.py:62
  31.9 483.7 %reduce-scatter.2.cloned.1.call-start = ((), (), s32[]{:S(2)}) async-start(), calls=%async_computation.4 | async-start | bytes 12976128 | tf_op jit(solution)/shard_map/reduce_scatter | solution.py:64
  277.9 342.6 %all-gather.2.cloned.1.call-start = ((), (), s32[]{:S(2)}) async-start(), calls=%async_computation.5 | async-start | bytes 6488064 | tf_op jit(solution)/shard_map/all_gather | solution.py:66
Sparse Core Ops, SparseCore 0:
  278.0 237.5 reduce-scatter.1
  530.4 90.0 all-gather.1
where the time goes:
time: 802 us; the launch traced here: 800 us
  waiting for transfers between devices  515 us (64%)
  local copies, waits for them, and re-layouts  126 us (16%)
  blocking collectives  71.4 us (9%)
  matrix products  36.8 us (5%)
  other arithmetic  24.2 us (3%)
  between operations  13.7 us (2%)
  starting transfers between devices  12.5 us (2%)
    reduce_scatter x1, waiting for transfers between devices, on_device(): lax.psum_scatter(block_gram(anchors, columns), 'expert', scatter_dimensio...  237 us
    all_to_all x1, waiting for transfers between devices, on_device(): lax.all_to_all(w_up, 'expert', split_axis=2, concat_axis=0, tiled=True)  188 us
    all_gather x1, waiting for transfers between devices, on_device(): lax.all_gather(polar, 'expert', axis=0, tiled=True)  90.1 us
    all_to_all x1, blocking collectives, on_device(): lax.all_to_all(merged, 'expert', split_axis=0, concat_axis=2, tiled=True)  41.9 us
    unnamed x10, local copies, waits for them, and re-layouts  31.6 us
    all_to_all x1, blocking collectives, on_device(): lax.all_to_all(lax.all_to_all(merged, 'expert', split_axis=0, concat_axis...  29.5 us
    unnamed x1, other arithmetic  23.6 us
  transfers between devices with their start and end apart: 3, of which 3 were waited for; matrix products, arithmetic and copies ran while one was open for 0% of the time, Pallas kernels for 0%

commit v1 on v0

--- a/solution.py
+++ b/solution.py
@@ -63,7 +63,13 @@
     anchors = jnp.take(columns, anchor_of, axis=0)
     gram = lax.psum_scatter(block_gram(anchors, columns), "expert", scatter_dimension=0, tiled=True)
     polar = polar_factors(gram)
-    aligned = align_rows(lax.all_gather(polar, "expert", axis=0, tiled=True), columns, weight)
+    aligned = align_rows(
+        jnp.concatenate(
+            lax.all_to_all(jnp.stack([polar] * lax.axis_size("expert")), "expert", 0, 0), axis=0
+        ),
+        columns,
+        weight,
+    )
     select = member.astype(jnp.bfloat16)
     summed = jnp.dot(select, aligned.reshape(experts, -1), preferred_element_type=jnp.float32)
     merged = summed.reshape(clusters, aligned.shape[1], aligned.shape[2]).astype(jnp.bfloat16)

time: 802 us -> 849 us (1.059)
  waiting for transfers between devices: 515 us -> 564 us
  local copies, waits for them, and re-layouts: 126 us -> 115 us
    all_to_all x0 -> x1, waiting for transfers between devices: none -> 138 us  [on_device(): lax.all_to_all(jnp.stack([polar] * lax.axis_size('expert')), 'expert', 0, 0)]
    all_gather x1 -> x0, waiting for transfers between devices: 90.1 us -> none  [on_device(): lax.all_gather(polar, 'expert', axis=0, tiled=True)]
    reshape x2 -> x0, local copies, waits for them, and re-layouts: 9.31 us -> none  [the longest x1 8.49 us: align_rows(): turn = factors.reshape(experts, BLOCK, nblocks, BLOCK)]
    all_gather x1 -> x0, local copies, waits for them, and re-layouts: 8.78 us -> none  [on_device(): lax.all_gather(polar, 'expert', axis=0, tiled=True)]
where the time goes in v1:
time: 849 us; the launch traced here: 847 us
  waiting for transfers between devices  564 us (66%)
  local copies, waits for them, and re-layouts  115 us (14%)
  blocking collectives  71.2 us (8%)
  matrix products  40.8 us (5%)
  other arithmetic  24.2 us (3%)
  starting transfers between devices  19.2 us (2%)
  between operations  13.6 us (2%)
    reduce_scatter x1, waiting for transfers between devices, on_device(): lax.psum_scatter(block_gram(anchors, columns), 'expert', scatter_dimensio...  238 us
    all_to_all x1, waiting for transfers between devices, on_device(): lax.all_to_all(w_up, 'expert', split_axis=2, concat_axis=0, tiled=True)  188 us
    all_to_all x1, waiting for transfers between devices, on_device(): lax.all_to_all(jnp.stack([polar] * lax.axis_size('expert')), 'expert', 0, 0)  138 us
    all_to_all x1, blocking collectives, on_device(): lax.all_to_all(merged, 'expert', split_axis=0, concat_axis=2, tiled=True)  41 us
    unnamed x10, local copies, waits for them, and re-layouts  34.3 us
    all_to_all x1, blocking collectives, on_device(): lax.all_to_all(lax.all_to_all(merged, 'expert', split_axis=0, concat_axis...  30.2 us
    unnamed x1, other arithmetic  23.6 us
  transfers between devices with their start and end apart: 3, of which 3 were waited for; matrix products, arithmetic and copies ran while one was open for 0% of the time, Pallas kernels for 0%

profile of v1, /device:TPU:1, one launch (start us, length us, event | category | flops | bytes accessed | tf_op | source)
XLA Modules:
  0.0 847.2 jit_solution(5308956048008398351)
XLA Ops:
  6.5 13.1 %copy.39 = bf16[4,192,4096]{1,0,2:T(4,128)(2,1)} copy(bf16[4,192,4096]{2,1,0:T(8,128)(2,1)} %param.3) | data formatting | bytes 12582912 | tf_op args[0]
  19.6 12.3 %all-to-all-start = ((bf16[4,192,4096]{1,0,2:T(4,128)(2,1)}), bf16[4,192,4096]{1,0,2:T(4,128)(2,1)}, u32[]{:S(2)}, u32[]{:S(2)}) async-start(bf16[4,192,4096]{1,0,2:T(4,128)(2,1)} %copy.39), calls=%async_computation | async-start | bytes 16777216 | tf_op jit(solution)/shard_map/all_to_all | solution.py:62
  32.3 187.8 %all-to-all-done = bf16[4,192,4096]{1,0,2:T(4,128)(2,1)} async-done(((bf16[4,192,4096]{1,0,2:T(4,128)(2,1)}), bf16[4,192,4096]{1,0,2:T(4,128)(2,1)}, u32[]{:S(2)}, u32[]{:S(2)}) %all-to-all-start) | async-done | bytes 6291488 | tf_op jit(solution)/shard_map/all_to_all | solution.py:62
  220.1 13.2 %copy.40 = bf16[4,192,32,128]{3,1,0,2:T(8,128)(2,1)} copy(bf16[4,192,32,128]{1,0,3,2:T(4,128)(2,1)} %bitcast.2) | data formatting | bytes 12582912 | tf_op jit(solution)/shard_map/all_to_all | solution.py:62
  233.3 6.7 gather_fusion
  240.0 13.4 %fusion.3 = f32[128,96,2,96]{3,1,2,0:T(8,128)} fusion(bf16[128,2,96,128]{3,2,1,0:T(8,128)(2,1)} %bitcast.128, bf16[128,2,96,128]{3,2,1,0:T(8,128)(2,1)} %bitcast.134, pred[128]{0:T(512)(128)(4,1)S(1)} %compare_and_fusion), kind=kOutput, calls=%fused_computation.6 | convolution fusion | flops 607125504 | bytes 22020224 | tf_op jit(solution)/shard_map/nbid,nbjd->nibj/dot_general | solution.py:27
  253.5 11.7 %copy.41 = f32[128,96,2,96]{0,3,2,1:T(8,128)} copy(f32[128,96,2,96]{3,1,2,0:T(8,128)} %fusion.3) | data formatting | bytes 18874368 | tf_op jit(solution)/shard_map/nbid,nbjd->nibj/transpose | solution.py:27
  265.2 12.7 %copy.42 = f32[128,96,192]{2,1,0:T(8,128)} copy(f32[128,96,192]{0,2,1:T(8,128)} %bitcast.130) | data formatting | bytes 18874368 | tf_op jit(solution)/shard_map/reshape | solution.py:28
  277.9 237.7 %reduce-scatter.2.cloned.1.call-done = f32[4,96,192]{2,1,0:T(8,128)} async-done(((f32[128,96,192]{2,1,0:T(8,128)}), f32[4,96,192]{2,1,0:T(8,128)}) %reduce-scatter.2.cloned.1.call-update) | async-done | bytes 294928 | tf_op jit(solution)/shard_map/reduce_scatter | solution.py:64
  515.6 1.2 copy.43
  517.1 1.0 fusion.18
  520.2 0.9 fusion.34
  523.1 0.9 fusion.35
  524.6 0.9 fusion.38
  526.0 0.9 fusion.33
  527.5 1.0 fusion.21
  529.4 4.2 stack.3
  533.6 6.8 all-to-all-start.1
  540.6 138.1 %all-to-all-done.1 = bf16[32,4,96,192]{2,3,1,0:T(8,128)(2,1)} async-done(((bf16[32,4,96,192]{2,3,1,0:T(8,128)(2,1)}), bf16[32,4,96,192]{2,3,1,0:T(8,128)(2,1)}, u32[]{:S(2)}, u32[]{:S(2)}) %all-to-all-start.1) | async-done | bytes 4718624 | tf_op jit(solution)/shard_map/all_to_all | solution.py:68
  678.7 10.4 %multiply_convert_fusion = bf16[128,2,96,128]{3,2,1,0:T(8,128)(2,1)} fusion(f32[128]{0:T(128)S(1)} %convert_divide_fusion, bf16[128,96,2,96]{1,3,2,0:T(8,128)(2,1)} %bitcast.22, bf16[128,2,96,128]{3,2,1,0:T(8,128)(2,1)} %bitcast.129), kind=kOutput, calls=%fused_computation.1 | convolution fusion | flops 610271232 | bytes 17302016 | tf_op jit(solution)/shard_map/nibj,nbjd->nbid/dot_general | solution.py:44
  689.1 10.7 %copy.59 = bf16[16,8,192,128]{3,1,2,0:T(8,128)(2,1)} copy(bf16[16,8,192,128]{3,2,1,0:T(8,128)(2,1)} %bitcast.133) | data formatting | bytes 12582912
  699.8 8.6 %copy.47 = bf16[24576,128]{1,0:T(8,128)(2,1)} copy(bf16[24576,128]{0,1:T(8,128)(2,1)} %bitcast.131) | data formatting | bytes 12582912 | tf_op jit(solution)/shard_map/dot_general | solution.py:74
  708.4 5.0 convolution_convert_fusion
  714.0 41.0 %all_to_all.59 = bf16[32,192,128]{2,1,0:T(8,128)(2,1)} all-to-all(bf16[32,192,128]{2,1,0:T(8,128)(2,1)S(1)} %copy.48), channel_id=1, replica_groups=mesh['expert'=32,'unit'=8] {'expert'}, dimensions={0} | all-to-all | bytes 3145728 | tf_op jit(solution)/shard_map/all_to_all | solution.py:77
  755.0 3.1 copy.54
  758.2 6.2 reshape.78
  764.9 23.6 %reduce.1 = bf16[4096,192]{1,0:T(8,128)(2,1)S(1)} reduce(bf16[4096,1,192]{2,1,0:T(2,128)(2,1)} %bitcast.135, bf16[]{:T(256)} %broadcast.143), dimensions={1}, to_apply=%bitcast.99.reduce_sub_computation | reduce | bytes 3145730
  788.5 4.4 reshape.79
  792.9 30.2 %all_to_all.60 = bf16[8,2,49152]{2,1,0:T(2,128)(2,1)S(1)} all-to-all(bf16[8,2,49152]{2,1,0:T(2,128)(2,1)} %reshape.79), channel_id=1, replica_groups=mesh['expert'=32,'unit'=8] {'unit'}, dimensions={0} | all-to-all | bytes 3145728 | tf_op jit(solution)/shard_map/all_to_all | solution.py:76
  823.1 4.9 reshape.80
  828.0 9.9 %copy.51 = bf16[1,192,4096]{2,1,0:T(8,128)(2,1)S(1)} copy(bf16[1,192,4096]{1,0,2:T(2,128)(2,1)} %bitcast.136) | data formatting | bytes 3145728 | tf_op jit(solution)/shard_map/all_to_all | solution.py:76
  838.7 1.6 copy.52
  (34 shorter events, 9.2 us)
Async XLA Ops:
  19.6 12.3 %copy-start.1 = (s32[128]{0:T(128)S(1)}, s32[128]{0:T(128)}, u32[]{:S(2)}) copy-start(s32[128]{0:T(128)} %param.5) | copy-start | bytes 1540
  19.6 12.4 %copy-start = (s32[128,1]{0,1:T(1,128)S(1)}, s32[128,1]{0,1:T(1,128)}, u32[]{:S(2)}) copy-start(s32[128,1]{0,1:T(1,128)} %param.4) | copy-start | bytes 1540
  19.6 200.5 %all-to-all-start = ((bf16[4,192,4096]{1,0,2:T(4,128)(2,1)}), bf16[4,192,4096]{1,0,2:T(4,128)(2,1)}, u32[]{:S(2)}, u32[]{:S(2)}) async-start(bf16[4,192,4096]{1,0,2:T(4,128)(2,1)} %copy.39), calls=%async_computation | async-start | bytes 16777216 | tf_op jit(solution)/shard_map/all_to_all | solution.py:62
  31.9 483.7 %reduce-scatter.2.cloned.1.call-start = ((), (), s32[]{:S(2)}) async-start(), calls=%async_computation.5 | async-start | bytes 12976128 | tf_op jit(solution)/shard_map/reduce_scatter | solution.py:64
  533.6 145.1 %all-to-all-start.1 = ((bf16[32,4,96,192]{2,3,1,0:T(8,128)(2,1)}), bf16[32,4,96,192]{2,3,1,0:T(8,128)(2,1)}, u32[]{:S(2)}, u32[]{:S(2)}) async-start(bf16[32,4,96,192]{2,3,1,0:T(8,128)(2,1)} %stack.3), calls=%async_computation.2 | async-start | bytes 12582912 | tf_op jit(solution)/shard_map/all_to_all | solution.py:68
Sparse Core Ops, SparseCore 0:
  278.0 237.5 reduce-scatter.1
